TPU v7x, 32 devices: a whole 2x2x4 slice. The times are simulated.
32 devices in a mesh: groups: 2 (over x), hist: 16 (over z, y, core).
Axes of the slice: x: 2, y: 2, z: 4, core: 2. Of those that a mesh axis runs over, the one named last changes fastest.
Arguments:
- history: bfloat16 [16384, 1024], P(('groups', 'hist')), parts along dimension 0, may hold values from -6 to 6
- candidates: bfloat16 [512, 1024], P(('groups', 'hist')), parts along dimension 0, may hold values from -6 to 6
- hist_length: int32 [2], P('groups'), parts along dimension 0, may hold values from 4096 to 8192
- visible: int32 [512], P(('groups', 'hist')), parts along dimension 0, may hold values from 1 to 8192
- w_proj: bfloat16 [1024, 4096], replicated, may hold values from -0.1875 to 0.1875
- w_out: bfloat16 [1024, 1024], replicated, may hold values from -0.1875 to 0.1875
Outputs:
- scored: bfloat16 [512, 1024], P(('groups', 'hist')), parts along dimension 0
There are 2 independent parts, one for each index of `groups`. A program takes and returns all parts, laid end to end along the dimension named above; an argument that names none is the same for every part. Nothing has to cross between parts.
All inputs are finite; a program needn't handle non-finite values.
Results may differ from a plain program's by a relative error of at most 0.0022.
The roundings to bfloat16 on the way count: a program that leaves them out, or rounds other values in their place, can miss the bound.
Values may be sent and summed in bfloat16 or wider, within the bound.
A program may use at most 64 MiB of HBM per device.

v0:
```python
import jax
import jax.numpy as jnp
from jax import lax
from jax.sharding import PartitionSpec as P

HEADS = 8


EPS = 1e-06


def shifted(shard, axis, by):
    size = lax.axis_size(axis)
    return lax.ppermute(shard, axis, [(i, (i + by) % size) for i in range(size)])


def layer_norm(rows):
    rows = rows.astype(jnp.float32)
    centred = rows - jnp.mean(rows, axis=-1, keepdims=True)
    spread = jnp.mean(centred * centred, axis=-1, keepdims=True)
    return centred * lax.rsqrt(spread + EPS)


def attend(query, limit, keys, values, base, heads):
    rows = query.shape[0]
    n_keys = keys.shape[0]
    head_size = query.shape[1] // heads
    q_h = query.reshape(rows, heads, head_size)
    k_h = keys.reshape(n_keys, heads, head_size)
    v_h = values.reshape(n_keys, heads, head_size)
    scores = jnp.einsum("rhd,khd->hrk", q_h, k_h, preferred_element_type=jnp.float32)
    position = base + jnp.arange(n_keys, dtype=jnp.int32)
    seen = (position[None, :] < limit[:, None]).astype(jnp.float32)
    count = (limit + 1).astype(jnp.float32)
    weight = jax.nn.silu(scores * head_size ** (-0.5)) * seen[None] / count[None, :, None]
    weight = weight.astype(jnp.bfloat16)
    out = jnp.einsum("hrk,khd->rhd", weight, v_h, preferred_element_type=jnp.float32)
    return out.reshape(rows, -1)


def on_device(history, candidates, hist_length, visible, w_proj, w_out):
    width = w_out.shape[0]
    heads = HEADS
    head_size = width // heads
    hist_norm = layer_norm(history).astype(jnp.bfloat16)
    hist_kv = jax.nn.silu(
        jnp.dot(hist_norm, w_proj[:, 2 * width :], preferred_element_type=jnp.float32)
    ).astype(jnp.bfloat16)
    keys_local = hist_kv[:, :width]
    values_local = hist_kv[:, width:]
    cand_norm = layer_norm(candidates).astype(jnp.bfloat16)
    proj = jax.nn.silu(jnp.dot(cand_norm, w_proj, preferred_element_type=jnp.float32)).astype(
        jnp.bfloat16
    )
    gate = proj[:, :width]
    query = proj[:, width : 2 * width]
    self_key = proj[:, 2 * width : 3 * width]
    self_value = proj[:, 3 * width :]
    limit = jnp.minimum(visible, hist_length[0])
    count = (limit + 1).astype(jnp.float32)
    rows_here = query.shape[0]
    cycle_size = lax.axis_size("hist")
    base = lax.axis_index("hist") * history.shape[0]
    zeros = jnp.zeros((rows_here, width), jnp.float32)

    def turn(step, carry):
        query_now, limit_now, accum = carry
        accum = accum + attend(query_now, limit_now, keys_local, values_local, base, heads)
        return (
            shifted(query_now.astype(jnp.float32), "hist", 1).astype(query_now.dtype),
            shifted(limit_now, "hist", 1),
            shifted(accum, "hist", 1),
        )

    carried = lax.fori_loop(0, cycle_size, turn, (query, limit, zeros))
    attended = carried[2]
    self_scores = (
        (query.astype(jnp.float32) * self_key.astype(jnp.float32))
        .reshape(rows_here, heads, head_size)
        .sum(-1)
    )
    self_weight = (
        (jax.nn.silu(self_scores * head_size ** (-0.5)) / count[:, None])
        .astype(jnp.bfloat16)
        .astype(jnp.float32)
    )
    self_term = (
        self_weight[:, :, None]
        * self_value.astype(jnp.float32).reshape(rows_here, heads, head_size)
    ).reshape(rows_here, width)
    attended = attended + self_term
    mixed = (layer_norm(attended) * gate.astype(jnp.float32)).astype(jnp.bfloat16)
    result = candidates.astype(jnp.float32) + jnp.dot(
        mixed, w_out, preferred_element_type=jnp.float32
    )
    return result.astype(jnp.bfloat16)


def solution(mesh):
    in_specs = (
        P(("groups", "hist"), None),
        P(("groups", "hist"), None),
        P("groups"),
        P(("groups", "hist")),
        P(),
        P(),
    )
    out_specs = P(("groups", "hist"), None)
    return jax.shard_map(
        on_device, mesh=mesh, in_specs=in_specs, out_specs=out_specs, check_vma=False
    )
```

profile of v0, /device:TPU:0, one launch (start us, length us, event | category | flops | bytes accessed | tf_op | source)
XLA Modules:
  0.0 160.1 jit_solution(5999162046175047444)
XLA Ops:
  0.0 1.0 convert_reduce_fusion.1
  1.0 0.9 fusion.32
  2.0 4.8 %multiply_convert_fusion.1 = bf16[16,4096]{1,0:T(8,128)(2,1)S(1)} fusion(bf16[1024,4096]{1,0:T(8,128)(2,1)} %param.12, bf16[16,1024]{1,0:T(8,128)(2,1)} %param.9, f32[16]{0:T(128)S(1)} %add_rsqrt_fusion.2, f32[16]{0:T(128)S(1)} %broadcast_multiply_fusion.2), kind=kOutput, calls=%fused_computation.32 | convolution fusion | flops 134610944 | bytes 8552576 | tf_op jit(solution)/shard_map/dot_general | solution.py:52
  6.9 0.2 convert_reduce_fusion
  7.1 0.4 fusion.22
  7.5 0.6 copy-done.1
  8.2 2.8 %multiply_convert_fusion = bf16[512,2048]{1,0:T(8,128)(2,1)S(1)} fusion(bf16[1024,4096]{1,0:T(8,128)(2,1)S(1)} %copy-done.1, bf16[512,1024]{1,0:T(8,128)(2,1)S(1)} %copy-done.2, f32[512]{0:T(512)S(1)} %add_rsqrt_fusion, f32[512]{0:T(512)S(1)} %broadcast_multiply_fusion), kind=kOutput, calls=%fused_computation.19 | convolution fusion | flops 2154823680 | bytes 7344128 | tf_op jit(solution)/shard_map/dot_general | solution.py:47
  11.0 1.2 fusion.47
  12.9 143.1 %while.14 = (s32[]{:T(128)}, bf16[16,1024]{1,0:T(8,128)(2,1)S(1)}, s32[16]{0:T(128)S(1)}, f32[16,1024]{1,0:T(8,128)S(1)}, bf16[512,1024]{1,0:T(8,128)(2,1)}, /*i...) while((s32[]{:T(128)}, bf16[16,1024]{1,0:T(8,128)(2,1)S(1)}, s32[16]{0:T(128)S(1)}, ...), condition=%wide.region_5.6_spmd, body=%wide.region_4.5_spmd.sunk | while | flops 34112032 | bytes 2921297 | solution.py:75
  13.0 0.1 compare_convert_fusion.2
  13.1 1.8 %convolution_bitcast_fusion.2 = f32[8,2,8,128]{3,2,1,0:T(8,128)S(1)} fusion(f32[16]{0:T(128)S(1)} %add_convert_fusion.3, f32[16,512]{1,0:T(8,128)S(1)} %compare_convert_fusion.2, bf16[512,1024]{1,0:T(8,128)(2,1)S(1)} %get-tuple-element.128, bf16[512,1024]{1,0:T(8,128)(2,1)} %get-tuple-element.126, bf16[16,1024]{1,0:T(8,128)(2,1)S(1)} %copy.64), kind=kOutput, calls=%fused_computation.1.clone.1 | convolution fusion | flops 34078720 | bytes 2228288 | tf_op jit(solution)/shard_map/while/body/eval_jaxpr/hrk,khd->rhd/dot_general | solution.py:37
  14.9 0.5 collective-permute-start.2
  15.4 2.6 %collective-permute-start = (bf16[16,1024]{1,0:T(8,128)(2,1)S(1)}, bf16[16,1024]{1,0:T(8,128)(2,1)S(1)}, u32[]{:S(2)}, u32[]{:S(2)}) collective-permute-start(bf16[16,1024]{1,0:T(8,128)(2,1)S(1)} %copy.64), channel_id=1, source_target_pairs={{0,1},{1,2},{2,3},{3,4},{4,5},{5,6},{6,7},{7,8},{8,9},{9,10},{10,1... | collective-permute-start | bytes 98312 | tf_op jit(solution)/shard_map/while/body/eval_jaxpr/ppermute | solution.py:14
  18.1 5.6 %collective-permute-done.1 = s32[16]{0:T(128)S(1)} collective-permute-done((s32[16]{0:T(128)S(1)}, s32[16]{0:T(128)S(1)}, u32[]{:S(2)}, u32[]{:S(2)}) %collective-permute-start.1) | collective-permute-done | bytes 96 | tf_op jit(solution)/shard_map/while/body/eval_jaxpr/ppermute | solution.py:14
  23.8 0.1 compare_convert_fusion.2
  23.9 1.8 %convolution_bitcast_fusion.2 = f32[8,2,8,128]{3,2,1,0:T(8,128)S(1)} fusion(f32[16]{0:T(128)S(1)} %add_convert_fusion.3, f32[16,512]{1,0:T(8,128)S(1)} %compare_convert_fusion.2, bf16[512,1024]{1,0:T(8,128)(2,1)S(1)} %get-tuple-element.128, bf16[512,1024]{1,0:T(8,128)(2,1)} %get-tuple-element.126, bf16[16,1024]{1,0:T(8,128)(2,1)S(1)} %copy.64), kind=kOutput, calls=%fused_computation.1.clone.1 | convolution fusion | flops 34078720 | bytes 2228288 | tf_op jit(solution)/shard_map/while/body/eval_jaxpr/hrk,khd->rhd/dot_general | solution.py:37
  25.9 6.7 %collective-permute-done.1 = s32[16]{0:T(128)S(1)} collective-permute-done((s32[16]{0:T(128)S(1)}, s32[16]{0:T(128)S(1)}, u32[]{:S(2)}, u32[]{:S(2)}) %collective-permute-start.1) | collective-permute-done | bytes 96 | tf_op jit(solution)/shard_map/while/body/eval_jaxpr/ppermute | solution.py:14
  32.6 0.1 compare_convert_fusion.2
  32.7 1.8 %convolution_bitcast_fusion.2 = f32[8,2,8,128]{3,2,1,0:T(8,128)S(1)} fusion(f32[16]{0:T(128)S(1)} %add_convert_fusion.3, f32[16,512]{1,0:T(8,128)S(1)} %compare_convert_fusion.2, bf16[512,1024]{1,0:T(8,128)(2,1)S(1)} %get-tuple-element.128, bf16[512,1024]{1,0:T(8,128)(2,1)} %get-tuple-element.126, bf16[16,1024]{1,0:T(8,128)(2,1)S(1)} %copy.64), kind=kOutput, calls=%fused_computation.1.clone.1 | convolution fusion | flops 34078720 | bytes 2228288 | tf_op jit(solution)/shard_map/while/body/eval_jaxpr/hrk,khd->rhd/dot_general | solution.py:37
  34.7 6.7 %collective-permute-done.1 = s32[16]{0:T(128)S(1)} collective-permute-done((s32[16]{0:T(128)S(1)}, s32[16]{0:T(128)S(1)}, u32[]{:S(2)}, u32[]{:S(2)}) %collective-permute-start.1) | collective-permute-done | bytes 96 | tf_op jit(solution)/shard_map/while/body/eval_jaxpr/ppermute | solution.py:14
  41.4 0.1 compare_convert_fusion.2
  41.5 1.8 %convolution_bitcast_fusion.2 = f32[8,2,8,128]{3,2,1,0:T(8,128)S(1)} fusion(f32[16]{0:T(128)S(1)} %add_convert_fusion.3, f32[16,512]{1,0:T(8,128)S(1)} %compare_convert_fusion.2, bf16[512,1024]{1,0:T(8,128)(2,1)S(1)} %get-tuple-element.128, bf16[512,1024]{1,0:T(8,128)(2,1)} %get-tuple-element.126, bf16[16,1024]{1,0:T(8,128)(2,1)S(1)} %copy.64), kind=kOutput, calls=%fused_computation.1.clone.1 | convolution fusion | flops 34078720 | bytes 2228288 | tf_op jit(solution)/shard_map/while/body/eval_jaxpr/hrk,khd->rhd/dot_general | solution.py:37
  43.5 6.7 %collective-permute-done.1 = s32[16]{0:T(128)S(1)} collective-permute-done((s32[16]{0:T(128)S(1)}, s32[16]{0:T(128)S(1)}, u32[]{:S(2)}, u32[]{:S(2)}) %collective-permute-start.1) | collective-permute-done | bytes 96 | tf_op jit(solution)/shard_map/while/body/eval_jaxpr/ppermute | solution.py:14
  50.2 0.1 compare_convert_fusion.2
  50.3 1.8 %convolution_bitcast_fusion.2 = f32[8,2,8,128]{3,2,1,0:T(8,128)S(1)} fusion(f32[16]{0:T(128)S(1)} %add_convert_fusion.3, f32[16,512]{1,0:T(8,128)S(1)} %compare_convert_fusion.2, bf16[512,1024]{1,0:T(8,128)(2,1)S(1)} %get-tuple-element.128, bf16[512,1024]{1,0:T(8,128)(2,1)} %get-tuple-element.126, bf16[16,1024]{1,0:T(8,128)(2,1)S(1)} %copy.64), kind=kOutput, calls=%fused_computation.1.clone.1 | convolution fusion | flops 34078720 | bytes 2228288 | tf_op jit(solution)/shard_map/while/body/eval_jaxpr/hrk,khd->rhd/dot_general | solution.py:37
  52.3 6.7 %collective-permute-done.1 = s32[16]{0:T(128)S(1)} collective-permute-done((s32[16]{0:T(128)S(1)}, s32[16]{0:T(128)S(1)}, u32[]{:S(2)}, u32[]{:S(2)}) %collective-permute-start.1) | collective-permute-done | bytes 96 | tf_op jit(solution)/shard_map/while/body/eval_jaxpr/ppermute | solution.py:14
  59.1 0.1 compare_convert_fusion.2
  59.1 1.8 %convolution_bitcast_fusion.2 = f32[8,2,8,128]{3,2,1,0:T(8,128)S(1)} fusion(f32[16]{0:T(128)S(1)} %add_convert_fusion.3, f32[16,512]{1,0:T(8,128)S(1)} %compare_convert_fusion.2, bf16[512,1024]{1,0:T(8,128)(2,1)S(1)} %get-tuple-element.128, bf16[512,1024]{1,0:T(8,128)(2,1)} %get-tuple-element.126, bf16[16,1024]{1,0:T(8,128)(2,1)S(1)} %copy.64), kind=kOutput, calls=%fused_computation.1.clone.1 | convolution fusion | flops 34078720 | bytes 2228288 | tf_op jit(solution)/shard_map/while/body/eval_jaxpr/hrk,khd->rhd/dot_general | solution.py:37
  61.2 6.7 %collective-permute-done.1 = s32[16]{0:T(128)S(1)} collective-permute-done((s32[16]{0:T(128)S(1)}, s32[16]{0:T(128)S(1)}, u32[]{:S(2)}, u32[]{:S(2)}) %collective-permute-start.1) | collective-permute-done | bytes 96 | tf_op jit(solution)/shard_map/while/body/eval_jaxpr/ppermute | solution.py:14
  67.9 0.1 compare_convert_fusion.2
  67.9 1.8 %convolution_bitcast_fusion.2 = f32[8,2,8,128]{3,2,1,0:T(8,128)S(1)} fusion(f32[16]{0:T(128)S(1)} %add_convert_fusion.3, f32[16,512]{1,0:T(8,128)S(1)} %compare_convert_fusion.2, bf16[512,1024]{1,0:T(8,128)(2,1)S(1)} %get-tuple-element.128, bf16[512,1024]{1,0:T(8,128)(2,1)} %get-tuple-element.126, bf16[16,1024]{1,0:T(8,128)(2,1)S(1)} %copy.64), kind=kOutput, calls=%fused_computation.1.clone.1 | convolution fusion | flops 34078720 | bytes 2228288 | tf_op jit(solution)/shard_map/while/body/eval_jaxpr/hrk,khd->rhd/dot_general | solution.py:37
  70.0 6.7 %collective-permute-done.1 = s32[16]{0:T(128)S(1)} collective-permute-done((s32[16]{0:T(128)S(1)}, s32[16]{0:T(128)S(1)}, u32[]{:S(2)}, u32[]{:S(2)}) %collective-permute-start.1) | collective-permute-done | bytes 96 | tf_op jit(solution)/shard_map/while/body/eval_jaxpr/ppermute | solution.py:14
  76.7 0.1 compare_convert_fusion.2
  76.8 1.8 %convolution_bitcast_fusion.2 = f32[8,2,8,128]{3,2,1,0:T(8,128)S(1)} fusion(f32[16]{0:T(128)S(1)} %add_convert_fusion.3, f32[16,512]{1,0:T(8,128)S(1)} %compare_convert_fusion.2, bf16[512,1024]{1,0:T(8,128)(2,1)S(1)} %get-tuple-element.128, bf16[512,1024]{1,0:T(8,128)(2,1)} %get-tuple-element.126, bf16[16,1024]{1,0:T(8,128)(2,1)S(1)} %copy.64), kind=kOutput, calls=%fused_computation.1.clone.1 | convolution fusion | flops 34078720 | bytes 2228288 | tf_op jit(solution)/shard_map/while/body/eval_jaxpr/hrk,khd->rhd/dot_general | solution.py:37
  78.8 6.7 %collective-permute-done.1 = s32[16]{0:T(128)S(1)} collective-permute-done((s32[16]{0:T(128)S(1)}, s32[16]{0:T(128)S(1)}, u32[]{:S(2)}, u32[]{:S(2)}) %collective-permute-start.1) | collective-permute-done | bytes 96 | tf_op jit(solution)/shard_map/while/body/eval_jaxpr/ppermute | solution.py:14
  85.5 0.1 compare_convert_fusion.2
  85.6 1.8 %convolution_bitcast_fusion.2 = f32[8,2,8,128]{3,2,1,0:T(8,128)S(1)} fusion(f32[16]{0:T(128)S(1)} %add_convert_fusion.3, f32[16,512]{1,0:T(8,128)S(1)} %compare_convert_fusion.2, bf16[512,1024]{1,0:T(8,128)(2,1)S(1)} %get-tuple-element.128, bf16[512,1024]{1,0:T(8,128)(2,1)} %get-tuple-element.126, bf16[16,1024]{1,0:T(8,128)(2,1)S(1)} %copy.64), kind=kOutput, calls=%fused_computation.1.clone.1 | convolution fusion | flops 34078720 | bytes 2228288 | tf_op jit(solution)/shard_map/while/body/eval_jaxpr/hrk,khd->rhd/dot_general | solution.py:37
  87.6 6.7 %collective-permute-done.1 = s32[16]{0:T(128)S(1)} collective-permute-done((s32[16]{0:T(128)S(1)}, s32[16]{0:T(128)S(1)}, u32[]{:S(2)}, u32[]{:S(2)}) %collective-permute-start.1) | collective-permute-done | bytes 96 | tf_op jit(solution)/shard_map/while/body/eval_jaxpr/ppermute | solution.py:14
  94.3 0.1 compare_convert_fusion.2
  94.4 1.8 %convolution_bitcast_fusion.2 = f32[8,2,8,128]{3,2,1,0:T(8,128)S(1)} fusion(f32[16]{0:T(128)S(1)} %add_convert_fusion.3, f32[16,512]{1,0:T(8,128)S(1)} %compare_convert_fusion.2, bf16[512,1024]{1,0:T(8,128)(2,1)S(1)} %get-tuple-element.128, bf16[512,1024]{1,0:T(8,128)(2,1)} %get-tuple-element.126, bf16[16,1024]{1,0:T(8,128)(2,1)S(1)} %copy.64), kind=kOutput, calls=%fused_computation.1.clone.1 | convolution fusion | flops 34078720 | bytes 2228288 | tf_op jit(solution)/shard_map/while/body/eval_jaxpr/hrk,khd->rhd/dot_general | solution.py:37
  96.4 6.7 %collective-permute-done.1 = s32[16]{0:T(128)S(1)} collective-permute-done((s32[16]{0:T(128)S(1)}, s32[16]{0:T(128)S(1)}, u32[]{:S(2)}, u32[]{:S(2)}) %collective-permute-start.1) | collective-permute-done | bytes 96 | tf_op jit(solution)/shard_map/while/body/eval_jaxpr/ppermute | solution.py:14
  103.1 0.1 compare_convert_fusion.2
  103.2 1.8 %convolution_bitcast_fusion.2 = f32[8,2,8,128]{3,2,1,0:T(8,128)S(1)} fusion(f32[16]{0:T(128)S(1)} %add_convert_fusion.3, f32[16,512]{1,0:T(8,128)S(1)} %compare_convert_fusion.2, bf16[512,1024]{1,0:T(8,128)(2,1)S(1)} %get-tuple-element.128, bf16[512,1024]{1,0:T(8,128)(2,1)} %get-tuple-element.126, bf16[16,1024]{1,0:T(8,128)(2,1)S(1)} %copy.64), kind=kOutput, calls=%fused_computation.1.clone.1 | convolution fusion | flops 34078720 | bytes 2228288 | tf_op jit(solution)/shard_map/while/body/eval_jaxpr/hrk,khd->rhd/dot_general | solution.py:37
  105.2 6.7 %collective-permute-done.1 = s32[16]{0:T(128)S(1)} collective-permute-done((s32[16]{0:T(128)S(1)}, s32[16]{0:T(128)S(1)}, u32[]{:S(2)}, u32[]{:S(2)}) %collective-permute-start.1) | collective-permute-done | bytes 96 | tf_op jit(solution)/shard_map/while/body/eval_jaxpr/ppermute | solution.py:14
  112.0 1.8 %convolution_bitcast_fusion.2 = f32[8,2,8,128]{3,2,1,0:T(8,128)S(1)} fusion(f32[16]{0:T(128)S(1)} %add_convert_fusion.3, f32[16,512]{1,0:T(8,128)S(1)} %compare_convert_fusion.2, bf16[512,1024]{1,0:T(8,128)(2,1)S(1)} %get-tuple-element.128, bf16[512,1024]{1,0:T(8,128)(2,1)} %get-tuple-element.126, bf16[16,1024]{1,0:T(8,128)(2,1)S(1)} %copy.64), kind=kOutput, calls=%fused_computation.1.clone.1 | convolution fusion | flops 34078720 | bytes 2228288 | tf_op jit(solution)/shard_map/while/body/eval_jaxpr/hrk,khd->rhd/dot_general | solution.py:37
  114.0 6.7 %collective-permute-done.1 = s32[16]{0:T(128)S(1)} collective-permute-done((s32[16]{0:T(128)S(1)}, s32[16]{0:T(128)S(1)}, u32[]{:S(2)}, u32[]{:S(2)}) %collective-permute-start.1) | collective-permute-done | bytes 96 | tf_op jit(solution)/shard_map/while/body/eval_jaxpr/ppermute | solution.py:14
  120.8 0.1 compare_convert_fusion.2
  120.8 1.8 %convolution_bitcast_fusion.2 = f32[8,2,8,128]{3,2,1,0:T(8,128)S(1)} fusion(f32[16]{0:T(128)S(1)} %add_convert_fusion.3, f32[16,512]{1,0:T(8,128)S(1)} %compare_convert_fusion.2, bf16[512,1024]{1,0:T(8,128)(2,1)S(1)} %get-tuple-element.128, bf16[512,1024]{1,0:T(8,128)(2,1)} %get-tuple-element.126, bf16[16,1024]{1,0:T(8,128)(2,1)S(1)} %copy.64), kind=kOutput, calls=%fused_computation.1.clone.1 | convolution fusion | flops 34078720 | bytes 2228288 | tf_op jit(solution)/shard_map/while/body/eval_jaxpr/hrk,khd->rhd/dot_general | solution.py:37
  122.9 6.7 %collective-permute-done.1 = s32[16]{0:T(128)S(1)} collective-permute-done((s32[16]{0:T(128)S(1)}, s32[16]{0:T(128)S(1)}, u32[]{:S(2)}, u32[]{:S(2)}) %collective-permute-start.1) | collective-permute-done | bytes 96 | tf_op jit(solution)/shard_map/while/body/eval_jaxpr/ppermute | solution.py:14
  129.6 0.1 compare_convert_fusion.2
  129.7 1.8 %convolution_bitcast_fusion.2 = f32[8,2,8,128]{3,2,1,0:T(8,128)S(1)} fusion(f32[16]{0:T(128)S(1)} %add_convert_fusion.3, f32[16,512]{1,0:T(8,128)S(1)} %compare_convert_fusion.2, bf16[512,1024]{1,0:T(8,128)(2,1)S(1)} %get-tuple-element.128, bf16[512,1024]{1,0:T(8,128)(2,1)} %get-tuple-element.126, bf16[16,1024]{1,0:T(8,128)(2,1)S(1)} %copy.64), kind=kOutput, calls=%fused_computation.1.clone.1 | convolution fusion | flops 34078720 | bytes 2228288 | tf_op jit(solution)/shard_map/while/body/eval_jaxpr/hrk,khd->rhd/dot_general | solution.py:37
  131.7 6.7 %collective-permute-done.1 = s32[16]{0:T(128)S(1)} collective-permute-done((s32[16]{0:T(128)S(1)}, s32[16]{0:T(128)S(1)}, u32[]{:S(2)}, u32[]{:S(2)}) %collective-permute-start.1) | collective-permute-done | bytes 96 | tf_op jit(solution)/shard_map/while/body/eval_jaxpr/ppermute | solution.py:14
  138.4 0.1 compare_convert_fusion.2
  138.5 1.8 %convolution_bitcast_fusion.2 = f32[8,2,8,128]{3,2,1,0:T(8,128)S(1)} fusion(f32[16]{0:T(128)S(1)} %add_convert_fusion.3, f32[16,512]{1,0:T(8,128)S(1)} %compare_convert_fusion.2, bf16[512,1024]{1,0:T(8,128)(2,1)S(1)} %get-tuple-element.128, bf16[512,1024]{1,0:T(8,128)(2,1)} %get-tuple-element.126, bf16[16,1024]{1,0:T(8,128)(2,1)S(1)} %copy.64), kind=kOutput, calls=%fused_computation.1.clone.1 | convolution fusion | flops 34078720 | bytes 2228288 | tf_op jit(solution)/shard_map/while/body/eval_jaxpr/hrk,khd->rhd/dot_general | solution.py:37
  140.5 6.7 %collective-permute-done.1 = s32[16]{0:T(128)S(1)} collective-permute-done((s32[16]{0:T(128)S(1)}, s32[16]{0:T(128)S(1)}, u32[]{:S(2)}, u32[]{:S(2)}) %collective-permute-start.1) | collective-permute-done | bytes 96 | tf_op jit(solution)/shard_map/while/body/eval_jaxpr/ppermute | solution.py:14
  147.3 1.8 %convolution_bitcast_fusion.2 = f32[8,2,8,128]{3,2,1,0:T(8,128)S(1)} fusion(f32[16]{0:T(128)S(1)} %add_convert_fusion.3, f32[16,512]{1,0:T(8,128)S(1)} %compare_convert_fusion.2, bf16[512,1024]{1,0:T(8,128)(2,1)S(1)} %get-tuple-element.128, bf16[512,1024]{1,0:T(8,128)(2,1)} %get-tuple-element.126, bf16[16,1024]{1,0:T(8,128)(2,1)S(1)} %copy.64), kind=kOutput, calls=%fused_computation.1.clone.1 | convolution fusion | flops 34078720 | bytes 2228288 | tf_op jit(solution)/shard_map/while/body/eval_jaxpr/hrk,khd->rhd/dot_general | solution.py:37
  149.3 6.7 %collective-permute-done.1 = s32[16]{0:T(128)S(1)} collective-permute-done((s32[16]{0:T(128)S(1)}, s32[16]{0:T(128)S(1)}, u32[]{:S(2)}, u32[]{:S(2)}) %collective-permute-start.1) | collective-permute-done | bytes 96 | tf_op jit(solution)/shard_map/while/body/eval_jaxpr/ppermute | solution.py:14
  156.0 0.8 multiply_bitcast_fusion
  156.8 0.1 reduce_sum.67
  157.0 0.1 copy.24
  157.1 0.1 mul.107
  157.1 0.9 fusion.45
  158.1 0.2 multiply_reduce_fusion
  158.3 1.8 %fusion.26 = bf16[16,1024]{1,0:T(8,128)(2,1)} fusion(bf16[1024,1024]{1,0:T(8,128)(2,1)S(1)} %copy-done, bf16[16,1024]{1,0:T(8,128)(2,1)S(1)} %copy-done.3, f32[16,1024]{1,0:T(8,128)S(1)} %get-tuple-element.58, bf16[16,4096]{1,0:T(8,128)(2,1)} %copy-done.4, f32[16]{0:T(128)S(1)} %add_rsqrt_fusion.1, f32[16]{0:T(128)S(1)} %broadcast_multiply_fusion.1), kind=kOutput, calls=%fused_computation.29 | convolution fusion | flops 33685504 | bytes 2261120 | tf_op jit(solution)/shard_map/dot_general | solution.py:93
  (183 shorter events, 3.6 us)
Async XLA Ops:
  0.0 158.3 %copy-start = (bf16[1024,1024]{1,0:T(8,128)(2,1)S(1)}, bf16[1024,1024]{1,0:T(8,128)(2,1)}, u32[]{:S(2)}) copy-start(bf16[1024,1024]{1,0:T(8,128)(2,1)} %param.13) | copy-start | bytes 6291460
  2.0 4.9 %copy-start.2 = (bf16[512,1024]{1,0:T(8,128)(2,1)S(1)}, bf16[512,1024]{1,0:T(8,128)(2,1)}, u32[]{:S(2)}) copy-start(bf16[512,1024]{1,0:T(8,128)(2,1)} %param.8) | copy-start | bytes 3145732
  2.0 6.2 %copy-start.1 = (bf16[1024,4096]{1,0:T(8,128)(2,1)S(1)}, bf16[1024,4096]{1,0:T(8,128)(2,1)}, u32[]{:S(2)}) copy-start(bf16[1024,4096]{1,0:T(8,128)(2,1)} %param.12) | copy-start | bytes 25165828
  6.8 0.7 copy-start.4
  11.0 1.9 %copy-start.5 = (s32[16]{0:T(128)S(1)}, s32[16]{0:T(128)}, u32[]{:S(2)}) copy-start(s32[16]{0:T(128)} %param.11) | copy-start | bytes 196
  12.9 145.3 %copy-start.3 = (bf16[16,1024]{1,0:T(8,128)(2,1)S(1)}, bf16[16,1024]{1,0:T(8,128)(2,1)}, u32[]{:S(2)}) copy-start(bf16[16,1024]{1,0:T(8,128)(2,1)} %param.9) | copy-start | bytes 98308
  14.9 8.9 %collective-permute-start.2 = (f32[16,1024]{1,0:T(8,128)S(1)}, f32[16,1024]{1,0:T(8,128)S(1)}, u32[]{:S(2)}, u32[]{:S(2)}) collective-permute-start(f32[16,1024]{1,0:T(8,128)S(1)} %bitcast_add_fusion.2), channel_id=1, source_target_pairs={{0,1},{1,2},{2,3},{3,4},{4,5},{5,6},{6,7},{7,8},{8,9},{9,10},{10,1... | collective-permute-start | bytes 196616 | tf_op jit(solution)/shard_map/while/body/eval_jaxpr/ppermute | solution.py:14
  15.4 8.3 %collective-permute-start = (bf16[16,1024]{1,0:T(8,128)(2,1)S(1)}, bf16[16,1024]{1,0:T(8,128)(2,1)S(1)}, u32[]{:S(2)}, u32[]{:S(2)}) collective-permute-start(bf16[16,1024]{1,0:T(8,128)(2,1)S(1)} %copy.64), channel_id=1, source_target_pairs={{0,1},{1,2},{2,3},{3,4},{4,5},{5,6},{6,7},{7,8},{8,9},{9,10},{10,1... | collective-permute-start | bytes 98312 | tf_op jit(solution)/shard_map/while/body/eval_jaxpr/ppermute | solution.py:14
  18.1 5.7 %collective-permute-start.1 = (s32[16]{0:T(128)S(1)}, s32[16]{0:T(128)S(1)}, u32[]{:S(2)}, u32[]{:S(2)}) collective-permute-start(s32[16]{0:T(128)S(1)} %copy.65), channel_id=1, source_target_pairs={{0,1},{1,2},{2,3},{3,4},{4,5},{5,6},{6,7},{7,8},{8,9},{9,10},{10,1... | collective-permute-start | bytes 200 | tf_op jit(solution)/shard_map/while/body/eval_jaxpr/ppermute | solution.py:14
  25.7 6.9 %collective-permute-start.2 = (f32[16,1024]{1,0:T(8,128)S(1)}, f32[16,1024]{1,0:T(8,128)S(1)}, u32[]{:S(2)}, u32[]{:S(2)}) collective-permute-start(f32[16,1024]{1,0:T(8,128)S(1)} %bitcast_add_fusion.2), channel_id=1, source_target_pairs={{0,1},{1,2},{2,3},{3,4},{4,5},{5,6},{6,7},{7,8},{8,9},{9,10},{10,1... | collective-permute-start | bytes 196616 | tf_op jit(solution)/shard_map/while/body/eval_jaxpr/ppermute | solution.py:14
  25.8 6.8 %collective-permute-start = (bf16[16,1024]{1,0:T(8,128)(2,1)S(1)}, bf16[16,1024]{1,0:T(8,128)(2,1)S(1)}, u32[]{:S(2)}, u32[]{:S(2)}) collective-permute-start(bf16[16,1024]{1,0:T(8,128)(2,1)S(1)} %copy.64), channel_id=1, source_target_pairs={{0,1},{1,2},{2,3},{3,4},{4,5},{5,6},{6,7},{7,8},{8,9},{9,10},{10,1... | collective-permute-start | bytes 98312 | tf_op jit(solution)/shard_map/while/body/eval_jaxpr/ppermute | solution.py:14
  25.8 6.7 %collective-permute-start.1 = (s32[16]{0:T(128)S(1)}, s32[16]{0:T(128)S(1)}, u32[]{:S(2)}, u32[]{:S(2)}) collective-permute-start(s32[16]{0:T(128)S(1)} %copy.65), channel_id=1, source_target_pairs={{0,1},{1,2},{2,3},{3,4},{4,5},{5,6},{6,7},{7,8},{8,9},{9,10},{10,1... | collective-permute-start | bytes 200 | tf_op jit(solution)/shard_map/while/body/eval_jaxpr/ppermute | solution.py:14
  34.5 6.9 %collective-permute-start.2 = (f32[16,1024]{1,0:T(8,128)S(1)}, f32[16,1024]{1,0:T(8,128)S(1)}, u32[]{:S(2)}, u32[]{:S(2)}) collective-permute-start(f32[16,1024]{1,0:T(8,128)S(1)} %bitcast_add_fusion.2), channel_id=1, source_target_pairs={{0,1},{1,2},{2,3},{3,4},{4,5},{5,6},{6,7},{7,8},{8,9},{9,10},{10,1... | collective-permute-start | bytes 196616 | tf_op jit(solution)/shard_map/while/body/eval_jaxpr/ppermute | solution.py:14
  34.6 6.8 %collective-permute-start = (bf16[16,1024]{1,0:T(8,128)(2,1)S(1)}, bf16[16,1024]{1,0:T(8,128)(2,1)S(1)}, u32[]{:S(2)}, u32[]{:S(2)}) collective-permute-start(bf16[16,1024]{1,0:T(8,128)(2,1)S(1)} %copy.64), channel_id=1, source_target_pairs={{0,1},{1,2},{2,3},{3,4},{4,5},{5,6},{6,7},{7,8},{8,9},{9,10},{10,1... | collective-permute-start | bytes 98312 | tf_op jit(solution)/shard_map/while/body/eval_jaxpr/ppermute | solution.py:14
  34.6 6.7 %collective-permute-start.1 = (s32[16]{0:T(128)S(1)}, s32[16]{0:T(128)S(1)}, u32[]{:S(2)}, u32[]{:S(2)}) collective-permute-start(s32[16]{0:T(128)S(1)} %copy.65), channel_id=1, source_target_pairs={{0,1},{1,2},{2,3},{3,4},{4,5},{5,6},{6,7},{7,8},{8,9},{9,10},{10,1... | collective-permute-start | bytes 200 | tf_op jit(solution)/shard_map/while/body/eval_jaxpr/ppermute | solution.py:14
  43.3 6.9 %collective-permute-start.2 = (f32[16,1024]{1,0:T(8,128)S(1)}, f32[16,1024]{1,0:T(8,128)S(1)}, u32[]{:S(2)}, u32[]{:S(2)}) collective-permute-start(f32[16,1024]{1,0:T(8,128)S(1)} %bitcast_add_fusion.2), channel_id=1, source_target_pairs={{0,1},{1,2},{2,3},{3,4},{4,5},{5,6},{6,7},{7,8},{8,9},{9,10},{10,1... | collective-permute-start | bytes 196616 | tf_op jit(solution)/shard_map/while/body/eval_jaxpr/ppermute | solution.py:14
  43.4 6.8 %collective-permute-start = (bf16[16,1024]{1,0:T(8,128)(2,1)S(1)}, bf16[16,1024]{1,0:T(8,128)(2,1)S(1)}, u32[]{:S(2)}, u32[]{:S(2)}) collective-permute-start(bf16[16,1024]{1,0:T(8,128)(2,1)S(1)} %copy.64), channel_id=1, source_target_pairs={{0,1},{1,2},{2,3},{3,4},{4,5},{5,6},{6,7},{7,8},{8,9},{9,10},{10,1... | collective-permute-start | bytes 98312 | tf_op jit(solution)/shard_map/while/body/eval_jaxpr/ppermute | solution.py:14
  43.4 6.7 %collective-permute-start.1 = (s32[16]{0:T(128)S(1)}, s32[16]{0:T(128)S(1)}, u32[]{:S(2)}, u32[]{:S(2)}) collective-permute-start(s32[16]{0:T(128)S(1)} %copy.65), channel_id=1, source_target_pairs={{0,1},{1,2},{2,3},{3,4},{4,5},{5,6},{6,7},{7,8},{8,9},{9,10},{10,1... | collective-permute-start | bytes 200 | tf_op jit(solution)/shard_map/while/body/eval_jaxpr/ppermute | solution.py:14
  52.1 6.9 %collective-permute-start.2 = (f32[16,1024]{1,0:T(8,128)S(1)}, f32[16,1024]{1,0:T(8,128)S(1)}, u32[]{:S(2)}, u32[]{:S(2)}) collective-permute-start(f32[16,1024]{1,0:T(8,128)S(1)} %bitcast_add_fusion.2), channel_id=1, source_target_pairs={{0,1},{1,2},{2,3},{3,4},{4,5},{5,6},{6,7},{7,8},{8,9},{9,10},{10,1... | collective-permute-start | bytes 196616 | tf_op jit(solution)/shard_map/while/body/eval_jaxpr/ppermute | solution.py:14
  52.2 6.8 %collective-permute-start = (bf16[16,1024]{1,0:T(8,128)(2,1)S(1)}, bf16[16,1024]{1,0:T(8,128)(2,1)S(1)}, u32[]{:S(2)}, u32[]{:S(2)}) collective-permute-start(bf16[16,1024]{1,0:T(8,128)(2,1)S(1)} %copy.64), channel_id=1, source_target_pairs={{0,1},{1,2},{2,3},{3,4},{4,5},{5,6},{6,7},{7,8},{8,9},{9,10},{10,1... | collective-permute-start | bytes 98312 | tf_op jit(solution)/shard_map/while/body/eval_jaxpr/ppermute | solution.py:14
  52.3 6.7 %collective-permute-start.1 = (s32[16]{0:T(128)S(1)}, s32[16]{0:T(128)S(1)}, u32[]{:S(2)}, u32[]{:S(2)}) collective-permute-start(s32[16]{0:T(128)S(1)} %copy.65), channel_id=1, source_target_pairs={{0,1},{1,2},{2,3},{3,4},{4,5},{5,6},{6,7},{7,8},{8,9},{9,10},{10,1... | collective-permute-start | bytes 200 | tf_op jit(solution)/shard_map/while/body/eval_jaxpr/ppermute | solution.py:14
  60.9 6.9 %collective-permute-start.2 = (f32[16,1024]{1,0:T(8,128)S(1)}, f32[16,1024]{1,0:T(8,128)S(1)}, u32[]{:S(2)}, u32[]{:S(2)}) collective-permute-start(f32[16,1024]{1,0:T(8,128)S(1)} %bitcast_add_fusion.2), channel_id=1, source_target_pairs={{0,1},{1,2},{2,3},{3,4},{4,5},{5,6},{6,7},{7,8},{8,9},{9,10},{10,1... | collective-permute-start | bytes 196616 | tf_op jit(solution)/shard_map/while/body/eval_jaxpr/ppermute | solution.py:14
  61.0 6.8 %collective-permute-start = (bf16[16,1024]{1,0:T(8,128)(2,1)S(1)}, bf16[16,1024]{1,0:T(8,128)(2,1)S(1)}, u32[]{:S(2)}, u32[]{:S(2)}) collective-permute-start(bf16[16,1024]{1,0:T(8,128)(2,1)S(1)} %copy.64), channel_id=1, source_target_pairs={{0,1},{1,2},{2,3},{3,4},{4,5},{5,6},{6,7},{7,8},{8,9},{9,10},{10,1... | collective-permute-start | bytes 98312 | tf_op jit(solution)/shard_map/while/body/eval_jaxpr/ppermute | solution.py:14
  61.1 6.7 %collective-permute-start.1 = (s32[16]{0:T(128)S(1)}, s32[16]{0:T(128)S(1)}, u32[]{:S(2)}, u32[]{:S(2)}) collective-permute-start(s32[16]{0:T(128)S(1)} %copy.65), channel_id=1, source_target_pairs={{0,1},{1,2},{2,3},{3,4},{4,5},{5,6},{6,7},{7,8},{8,9},{9,10},{10,1... | collective-permute-start | bytes 200 | tf_op jit(solution)/shard_map/while/body/eval_jaxpr/ppermute | solution.py:14
  69.8 6.9 %collective-permute-start.2 = (f32[16,1024]{1,0:T(8,128)S(1)}, f32[16,1024]{1,0:T(8,128)S(1)}, u32[]{:S(2)}, u32[]{:S(2)}) collective-permute-start(f32[16,1024]{1,0:T(8,128)S(1)} %bitcast_add_fusion.2), channel_id=1, source_target_pairs={{0,1},{1,2},{2,3},{3,4},{4,5},{5,6},{6,7},{7,8},{8,9},{9,10},{10,1... | collective-permute-start | bytes 196616 | tf_op jit(solution)/shard_map/while/body/eval_jaxpr/ppermute | solution.py:14
  69.8 6.8 %collective-permute-start = (bf16[16,1024]{1,0:T(8,128)(2,1)S(1)}, bf16[16,1024]{1,0:T(8,128)(2,1)S(1)}, u32[]{:S(2)}, u32[]{:S(2)}) collective-permute-start(bf16[16,1024]{1,0:T(8,128)(2,1)S(1)} %copy.64), channel_id=1, source_target_pairs={{0,1},{1,2},{2,3},{3,4},{4,5},{5,6},{6,7},{7,8},{8,9},{9,10},{10,1... | collective-permute-start | bytes 98312 | tf_op jit(solution)/shard_map/while/body/eval_jaxpr/ppermute | solution.py:14
  69.9 6.7 %collective-permute-start.1 = (s32[16]{0:T(128)S(1)}, s32[16]{0:T(128)S(1)}, u32[]{:S(2)}, u32[]{:S(2)}) collective-permute-start(s32[16]{0:T(128)S(1)} %copy.65), channel_id=1, source_target_pairs={{0,1},{1,2},{2,3},{3,4},{4,5},{5,6},{6,7},{7,8},{8,9},{9,10},{10,1... | collective-permute-start | bytes 200 | tf_op jit(solution)/shard_map/while/body/eval_jaxpr/ppermute | solution.py:14
  78.6 6.9 %collective-permute-start.2 = (f32[16,1024]{1,0:T(8,128)S(1)}, f32[16,1024]{1,0:T(8,128)S(1)}, u32[]{:S(2)}, u32[]{:S(2)}) collective-permute-start(f32[16,1024]{1,0:T(8,128)S(1)} %bitcast_add_fusion.2), channel_id=1, source_target_pairs={{0,1},{1,2},{2,3},{3,4},{4,5},{5,6},{6,7},{7,8},{8,9},{9,10},{10,1... | collective-permute-start | bytes 196616 | tf_op jit(solution)/shard_map/while/body/eval_jaxpr/ppermute | solution.py:14
  78.6 6.8 %collective-permute-start = (bf16[16,1024]{1,0:T(8,128)(2,1)S(1)}, bf16[16,1024]{1,0:T(8,128)(2,1)S(1)}, u32[]{:S(2)}, u32[]{:S(2)}) collective-permute-start(bf16[16,1024]{1,0:T(8,128)(2,1)S(1)} %copy.64), channel_id=1, source_target_pairs={{0,1},{1,2},{2,3},{3,4},{4,5},{5,6},{6,7},{7,8},{8,9},{9,10},{10,1... | collective-permute-start | bytes 98312 | tf_op jit(solution)/shard_map/while/body/eval_jaxpr/ppermute | solution.py:14
  78.7 6.7 %collective-permute-start.1 = (s32[16]{0:T(128)S(1)}, s32[16]{0:T(128)S(1)}, u32[]{:S(2)}, u32[]{:S(2)}) collective-permute-start(s32[16]{0:T(128)S(1)} %copy.65), channel_id=1, source_target_pairs={{0,1},{1,2},{2,3},{3,4},{4,5},{5,6},{6,7},{7,8},{8,9},{9,10},{10,1... | collective-permute-start | bytes 200 | tf_op jit(solution)/shard_map/while/body/eval_jaxpr/ppermute | solution.py:14
  87.4 6.9 %collective-permute-start.2 = (f32[16,1024]{1,0:T(8,128)S(1)}, f32[16,1024]{1,0:T(8,128)S(1)}, u32[]{:S(2)}, u32[]{:S(2)}) collective-permute-start(f32[16,1024]{1,0:T(8,128)S(1)} %bitcast_add_fusion.2), channel_id=1, source_target_pairs={{0,1},{1,2},{2,3},{3,4},{4,5},{5,6},{6,7},{7,8},{8,9},{9,10},{10,1... | collective-permute-start | bytes 196616 | tf_op jit(solution)/shard_map/while/body/eval_jaxpr/ppermute | solution.py:14
  87.5 6.8 %collective-permute-start = (bf16[16,1024]{1,0:T(8,128)(2,1)S(1)}, bf16[16,1024]{1,0:T(8,128)(2,1)S(1)}, u32[]{:S(2)}, u32[]{:S(2)}) collective-permute-start(bf16[16,1024]{1,0:T(8,128)(2,1)S(1)} %copy.64), channel_id=1, source_target_pairs={{0,1},{1,2},{2,3},{3,4},{4,5},{5,6},{6,7},{7,8},{8,9},{9,10},{10,1... | collective-permute-start | bytes 98312 | tf_op jit(solution)/shard_map/while/body/eval_jaxpr/ppermute | solution.py:14
  87.5 6.7 %collective-permute-start.1 = (s32[16]{0:T(128)S(1)}, s32[16]{0:T(128)S(1)}, u32[]{:S(2)}, u32[]{:S(2)}) collective-permute-start(s32[16]{0:T(128)S(1)} %copy.65), channel_id=1, source_target_pairs={{0,1},{1,2},{2,3},{3,4},{4,5},{5,6},{6,7},{7,8},{8,9},{9,10},{10,1... | collective-permute-start | bytes 200 | tf_op jit(solution)/shard_map/while/body/eval_jaxpr/ppermute | solution.py:14
  96.2 6.9 %collective-permute-start.2 = (f32[16,1024]{1,0:T(8,128)S(1)}, f32[16,1024]{1,0:T(8,128)S(1)}, u32[]{:S(2)}, u32[]{:S(2)}) collective-permute-start(f32[16,1024]{1,0:T(8,128)S(1)} %bitcast_add_fusion.2), channel_id=1, source_target_pairs={{0,1},{1,2},{2,3},{3,4},{4,5},{5,6},{6,7},{7,8},{8,9},{9,10},{10,1... | collective-permute-start | bytes 196616 | tf_op jit(solution)/shard_map/while/body/eval_jaxpr/ppermute | solution.py:14
  96.3 6.8 %collective-permute-start = (bf16[16,1024]{1,0:T(8,128)(2,1)S(1)}, bf16[16,1024]{1,0:T(8,128)(2,1)S(1)}, u32[]{:S(2)}, u32[]{:S(2)}) collective-permute-start(bf16[16,1024]{1,0:T(8,128)(2,1)S(1)} %copy.64), channel_id=1, source_target_pairs={{0,1},{1,2},{2,3},{3,4},{4,5},{5,6},{6,7},{7,8},{8,9},{9,10},{10,1... | collective-permute-start | bytes 98312 | tf_op jit(solution)/shard_map/while/body/eval_jaxpr/ppermute | solution.py:14
  96.3 6.7 %collective-permute-start.1 = (s32[16]{0:T(128)S(1)}, s32[16]{0:T(128)S(1)}, u32[]{:S(2)}, u32[]{:S(2)}) collective-permute-start(s32[16]{0:T(128)S(1)} %copy.65), channel_id=1, source_target_pairs={{0,1},{1,2},{2,3},{3,4},{4,5},{5,6},{6,7},{7,8},{8,9},{9,10},{10,1... | collective-permute-start | bytes 200 | tf_op jit(solution)/shard_map/while/body/eval_jaxpr/ppermute | solution.py:14
  105.0 6.9 %collective-permute-start.2 = (f32[16,1024]{1,0:T(8,128)S(1)}, f32[16,1024]{1,0:T(8,128)S(1)}, u32[]{:S(2)}, u32[]{:S(2)}) collective-permute-start(f32[16,1024]{1,0:T(8,128)S(1)} %bitcast_add_fusion.2), channel_id=1, source_target_pairs={{0,1},{1,2},{2,3},{3,4},{4,5},{5,6},{6,7},{7,8},{8,9},{9,10},{10,1... | collective-permute-start | bytes 196616 | tf_op jit(solution)/shard_map/while/body/eval_jaxpr/ppermute | solution.py:14
  105.1 6.8 %collective-permute-start = (bf16[16,1024]{1,0:T(8,128)(2,1)S(1)}, bf16[16,1024]{1,0:T(8,128)(2,1)S(1)}, u32[]{:S(2)}, u32[]{:S(2)}) collective-permute-start(bf16[16,1024]{1,0:T(8,128)(2,1)S(1)} %copy.64), channel_id=1, source_target_pairs={{0,1},{1,2},{2,3},{3,4},{4,5},{5,6},{6,7},{7,8},{8,9},{9,10},{10,1... | collective-permute-start | bytes 98312 | tf_op jit(solution)/shard_map/while/body/eval_jaxpr/ppermute | solution.py:14
  105.2 6.7 %collective-permute-start.1 = (s32[16]{0:T(128)S(1)}, s32[16]{0:T(128)S(1)}, u32[]{:S(2)}, u32[]{:S(2)}) collective-permute-start(s32[16]{0:T(128)S(1)} %copy.65), channel_id=1, source_target_pairs={{0,1},{1,2},{2,3},{3,4},{4,5},{5,6},{6,7},{7,8},{8,9},{9,10},{10,1... | collective-permute-start | bytes 200 | tf_op jit(solution)/shard_map/while/body/eval_jaxpr/ppermute | solution.py:14
  113.8 6.9 %collective-permute-start.2 = (f32[16,1024]{1,0:T(8,128)S(1)}, f32[16,1024]{1,0:T(8,128)S(1)}, u32[]{:S(2)}, u32[]{:S(2)}) collective-permute-start(f32[16,1024]{1,0:T(8,128)S(1)} %bitcast_add_fusion.2), channel_id=1, source_target_pairs={{0,1},{1,2},{2,3},{3,4},{4,5},{5,6},{6,7},{7,8},{8,9},{9,10},{10,1... | collective-permute-start | bytes 196616 | tf_op jit(solution)/shard_map/while/body/eval_jaxpr/ppermute | solution.py:14
  113.9 6.8 %collective-permute-start = (bf16[16,1024]{1,0:T(8,128)(2,1)S(1)}, bf16[16,1024]{1,0:T(8,128)(2,1)S(1)}, u32[]{:S(2)}, u32[]{:S(2)}) collective-permute-start(bf16[16,1024]{1,0:T(8,128)(2,1)S(1)} %copy.64), channel_id=1, source_target_pairs={{0,1},{1,2},{2,3},{3,4},{4,5},{5,6},{6,7},{7,8},{8,9},{9,10},{10,1... | collective-permute-start | bytes 98312 | tf_op jit(solution)/shard_map/while/body/eval_jaxpr/ppermute | solution.py:14
  114.0 6.7 %collective-permute-start.1 = (s32[16]{0:T(128)S(1)}, s32[16]{0:T(128)S(1)}, u32[]{:S(2)}, u32[]{:S(2)}) collective-permute-start(s32[16]{0:T(128)S(1)} %copy.65), channel_id=1, source_target_pairs={{0,1},{1,2},{2,3},{3,4},{4,5},{5,6},{6,7},{7,8},{8,9},{9,10},{10,1... | collective-permute-start | bytes 200 | tf_op jit(solution)/shard_map/while/body/eval_jaxpr/ppermute | solution.py:14
  122.7 6.9 %collective-permute-start.2 = (f32[16,1024]{1,0:T(8,128)S(1)}, f32[16,1024]{1,0:T(8,128)S(1)}, u32[]{:S(2)}, u32[]{:S(2)}) collective-permute-start(f32[16,1024]{1,0:T(8,128)S(1)} %bitcast_add_fusion.2), channel_id=1, source_target_pairs={{0,1},{1,2},{2,3},{3,4},{4,5},{5,6},{6,7},{7,8},{8,9},{9,10},{10,1... | collective-permute-start | bytes 196616 | tf_op jit(solution)/shard_map/while/body/eval_jaxpr/ppermute | solution.py:14
  122.7 6.8 %collective-permute-start = (bf16[16,1024]{1,0:T(8,128)(2,1)S(1)}, bf16[16,1024]{1,0:T(8,128)(2,1)S(1)}, u32[]{:S(2)}, u32[]{:S(2)}) collective-permute-start(bf16[16,1024]{1,0:T(8,128)(2,1)S(1)} %copy.64), channel_id=1, source_target_pairs={{0,1},{1,2},{2,3},{3,4},{4,5},{5,6},{6,7},{7,8},{8,9},{9,10},{10,1... | collective-permute-start | bytes 98312 | tf_op jit(solution)/shard_map/while/body/eval_jaxpr/ppermute | solution.py:14
  122.8 6.7 %collective-permute-start.1 = (s32[16]{0:T(128)S(1)}, s32[16]{0:T(128)S(1)}, u32[]{:S(2)}, u32[]{:S(2)}) collective-permute-start(s32[16]{0:T(128)S(1)} %copy.65), channel_id=1, source_target_pairs={{0,1},{1,2},{2,3},{3,4},{4,5},{5,6},{6,7},{7,8},{8,9},{9,10},{10,1... | collective-permute-start | bytes 200 | tf_op jit(solution)/shard_map/while/body/eval_jaxpr/ppermute | solution.py:14
  131.5 6.9 %collective-permute-start.2 = (f32[16,1024]{1,0:T(8,128)S(1)}, f32[16,1024]{1,0:T(8,128)S(1)}, u32[]{:S(2)}, u32[]{:S(2)}) collective-permute-start(f32[16,1024]{1,0:T(8,128)S(1)} %bitcast_add_fusion.2), channel_id=1, source_target_pairs={{0,1},{1,2},{2,3},{3,4},{4,5},{5,6},{6,7},{7,8},{8,9},{9,10},{10,1... | collective-permute-start | bytes 196616 | tf_op jit(solution)/shard_map/while/body/eval_jaxpr/ppermute | solution.py:14
  131.5 6.8 %collective-permute-start = (bf16[16,1024]{1,0:T(8,128)(2,1)S(1)}, bf16[16,1024]{1,0:T(8,128)(2,1)S(1)}, u32[]{:S(2)}, u32[]{:S(2)}) collective-permute-start(bf16[16,1024]{1,0:T(8,128)(2,1)S(1)} %copy.64), channel_id=1, source_target_pairs={{0,1},{1,2},{2,3},{3,4},{4,5},{5,6},{6,7},{7,8},{8,9},{9,10},{10,1... | collective-permute-start | bytes 98312 | tf_op jit(solution)/shard_map/while/body/eval_jaxpr/ppermute | solution.py:14
  131.6 6.7 %collective-permute-start.1 = (s32[16]{0:T(128)S(1)}, s32[16]{0:T(128)S(1)}, u32[]{:S(2)}, u32[]{:S(2)}) collective-permute-start(s32[16]{0:T(128)S(1)} %copy.65), channel_id=1, source_target_pairs={{0,1},{1,2},{2,3},{3,4},{4,5},{5,6},{6,7},{7,8},{8,9},{9,10},{10,1... | collective-permute-start | bytes 200 | tf_op jit(solution)/shard_map/while/body/eval_jaxpr/ppermute | solution.py:14
  140.3 6.9 %collective-permute-start.2 = (f32[16,1024]{1,0:T(8,128)S(1)}, f32[16,1024]{1,0:T(8,128)S(1)}, u32[]{:S(2)}, u32[]{:S(2)}) collective-permute-start(f32[16,1024]{1,0:T(8,128)S(1)} %bitcast_add_fusion.2), channel_id=1, source_target_pairs={{0,1},{1,2},{2,3},{3,4},{4,5},{5,6},{6,7},{7,8},{8,9},{9,10},{10,1... | collective-permute-start | bytes 196616 | tf_op jit(solution)/shard_map/while/body/eval_jaxpr/ppermute | solution.py:14
  140.4 6.8 %collective-permute-start = (bf16[16,1024]{1,0:T(8,128)(2,1)S(1)}, bf16[16,1024]{1,0:T(8,128)(2,1)S(1)}, u32[]{:S(2)}, u32[]{:S(2)}) collective-permute-start(bf16[16,1024]{1,0:T(8,128)(2,1)S(1)} %copy.64), channel_id=1, source_target_pairs={{0,1},{1,2},{2,3},{3,4},{4,5},{5,6},{6,7},{7,8},{8,9},{9,10},{10,1... | collective-permute-start | bytes 98312 | tf_op jit(solution)/shard_map/while/body/eval_jaxpr/ppermute | solution.py:14
  140.4 6.7 %collective-permute-start.1 = (s32[16]{0:T(128)S(1)}, s32[16]{0:T(128)S(1)}, u32[]{:S(2)}, u32[]{:S(2)}) collective-permute-start(s32[16]{0:T(128)S(1)} %copy.65), channel_id=1, source_target_pairs={{0,1},{1,2},{2,3},{3,4},{4,5},{5,6},{6,7},{7,8},{8,9},{9,10},{10,1... | collective-permute-start | bytes 200 | tf_op jit(solution)/shard_map/while/body/eval_jaxpr/ppermute | solution.py:14
  149.1 6.9 %collective-permute-start.2 = (f32[16,1024]{1,0:T(8,128)S(1)}, f32[16,1024]{1,0:T(8,128)S(1)}, u32[]{:S(2)}, u32[]{:S(2)}) collective-permute-start(f32[16,1024]{1,0:T(8,128)S(1)} %bitcast_add_fusion.2), channel_id=1, source_target_pairs={{0,1},{1,2},{2,3},{3,4},{4,5},{5,6},{6,7},{7,8},{8,9},{9,10},{10,1... | collective-permute-start | bytes 196616 | tf_op jit(solution)/shard_map/while/body/eval_jaxpr/ppermute | solution.py:14
  149.2 6.8 %collective-permute-start = (bf16[16,1024]{1,0:T(8,128)(2,1)S(1)}, bf16[16,1024]{1,0:T(8,128)(2,1)S(1)}, u32[]{:S(2)}, u32[]{:S(2)}) collective-permute-start(bf16[16,1024]{1,0:T(8,128)(2,1)S(1)} %copy.64), channel_id=1, source_target_pairs={{0,1},{1,2},{2,3},{3,4},{4,5},{5,6},{6,7},{7,8},{8,9},{9,10},{10,1... | collective-permute-start | bytes 98312 | tf_op jit(solution)/shard_map/while/body/eval_jaxpr/ppermute | solution.py:14
  149.2 6.7 %collective-permute-start.1 = (s32[16]{0:T(128)S(1)}, s32[16]{0:T(128)S(1)}, u32[]{:S(2)}, u32[]{:S(2)}) collective-permute-start(s32[16]{0:T(128)S(1)} %copy.65), channel_id=1, source_target_pairs={{0,1},{1,2},{2,3},{3,4},{4,5},{5,6},{6,7},{7,8},{8,9},{9,10},{10,1... | collective-permute-start | bytes 200 | tf_op jit(solution)/shard_map/while/body/eval_jaxpr/ppermute | solution.py:14
where the time goes:
time: 161 us; the launch traced here: 160 us
  waiting for transfers between devices  106 us (66%)
  matrix products  38.2 us (24%)
  other arithmetic  6.28 us (4%)
  starting transfers between devices  5.84 us (4%)
  local copies, waits for them, and re-layouts  2.2 us (1%)
    ppermute x48, waiting for transfers between devices, shifted(): lax.ppermute(shard, axis, [(i, (i + by) % size) for i in range(size)])  106 us
    dot_general x16, matrix products, attend(): jnp.einsum('hrk,khd->rhd', weight, v_h, preferred_element_type=jnp.float32)  28.7 us
    ppermute x48, starting transfers between devices, shifted(): lax.ppermute(shard, axis, [(i, (i + by) % size) for i in range(size)])  5.84 us
    dot_general x1, matrix products, on_device(): jnp.dot(cand_norm, w_proj, preferred_element_type=jnp.float32)  4.81 us
  transfers between devices with their start and end apart: 48, of which 16 were waited for; matrix products, arithmetic and copies ran while one was open for 0% of the time, Pallas kernels for 0%

commit v1 on v0

v1 whole, which is shorter than its diff:
```python
import functools

import jax
import jax.numpy as jnp
from jax import lax
from jax.experimental import pallas as pl
from jax.experimental.pallas import tpu as pltpu
from jax.sharding import PartitionSpec as P

HEADS = 8
EPS = 1e-06
LANES = 128
MESH = pl.DeviceIdType.MESH
F32 = jnp.float32
BF16 = jnp.bfloat16


def layer_norm(rows):
    rows = rows.astype(F32)
    centred = rows - jnp.mean(rows, axis=-1, keepdims=True)
    spread = jnp.mean(centred * centred, axis=-1, keepdims=True)
    return centred * lax.rsqrt(spread + EPS)


def silu(x):
    half = x * 0.5
    return half * jnp.tanh(half) + half


def dot(a, b):
    return jnp.dot(a, b, preferred_element_type=F32)


def kernel(
    n, cols,
    hist_ref, cand_ref, length_ref, visible_ref, w_proj_ref, w_out_ref, out_ref,
    hist, w_kv, w_q, w_gate, w_out, xs, kv, xall, q_all, mask, send_c, recv_c,
    keep, send_d, recv_d, own, load_sem, kv_sem,
    ag_s, ag_r, fw_s, fw_r, rc_s, rc_r, rd_s, rd_r,
):
    chips = n // 2
    me = lax.axis_index("hist")
    chip, side = lax.div(me, 2), lax.rem(me, 2)
    sibling = 2 * chip + (1 - side)
    rows, width = cand_ref.shape
    keys = hist_ref.shape[0]
    half = chips * rows
    head = width // HEADS
    groups = width // cols
    heads_in = cols // head

    def ahead(d):
        return 2 * lax.rem(chip + d, chips) + side

    def behind(d):
        return 2 * lax.rem(chip + chips - d, chips) + side

    load_hist = pltpu.make_async_copy(hist_ref, hist, load_sem.at[0])
    load_hist.start()
    kv_loads = []
    for j in range(2 * groups):
        copy = pltpu.make_async_copy(
            w_proj_ref.at[:, pl.ds(2 * width + j * cols, cols)], w_kv.at[j], kv_sem.at[j]
        )
        copy.start()
        kv_loads.append(copy)
    loads = [
        pltpu.make_async_copy(w_proj_ref.at[:, pl.ds(0, width)], w_gate, load_sem.at[1]),
        pltpu.make_async_copy(w_proj_ref.at[:, pl.ds(width, width)], w_q, load_sem.at[2]),
        pltpu.make_async_copy(w_out_ref, w_out, load_sem.at[3]),
    ]
    for copy in loads:
        copy.start()

    barrier = pltpu.get_barrier_semaphore()
    pl.semaphore_signal(barrier, inc=1, device_id={"hist": sibling}, device_id_type=MESH)
    for d in range(1, chips):
        pl.semaphore_signal(barrier, inc=1, device_id={"hist": ahead(d)}, device_id_type=MESH)

    row = lax.broadcasted_iota(jnp.int32, (rows, LANES), 0)
    lane = lax.broadcasted_iota(jnp.int32, (rows, LANES), 1)
    limit = jnp.zeros((rows, LANES), jnp.int32)
    for r in range(rows):
        limit = jnp.where(row == r, jnp.minimum(visible_ref[r], length_ref[0]), limit)
    count = (limit[:, :1] + 1).astype(F32)
    parts = jnp.where(lane < LANES // 2, limit >> 8, limit & 255)
    cand_norm = layer_norm(cand_ref[...]).astype(BF16)
    xall[0, 0, :, :width] = cand_norm
    xall[0, 0, :, width:] = parts.astype(F32).astype(BF16)
    xs[pl.ds(keys, rows), :] = cand_norm

    pl.semaphore_wait(barrier, chips)

    def remote(src, dst, s, r, to):
        return pltpu.make_async_remote_copy(
            src_ref=src, dst_ref=dst, send_sem=s, recv_sem=r,
            device_id={"hist": to}, device_id_type=MESH,
        )

    gathers = [None] + [
        remote(xall.at[0, 0], xall.at[0, d], ag_s.at[d], ag_r.at[d], ahead(d))
        for d in range(1, chips)
    ]
    forwards = [
        remote(xall.at[0, d], xall.at[1, d], fw_s.at[d], fw_r.at[d], sibling)
        for d in range(chips)
    ]
    for d in range(1, chips):
        gathers[d].start()
    forwards[0].start()

    load_hist.wait()
    for r in range(0, keys, LANES):
        xs[pl.ds(r, LANES), :] = layer_norm(hist[pl.ds(r, LANES), :]).astype(BF16)
    for j in range(2 * groups):
        kv_loads[j].wait()
        kv[j] = silu(dot(xs[...], w_kv[j])).astype(BF16)

    loads[0].wait()
    gate = silu(dot(xs[pl.ds(keys, rows), :], w_gate[...])).astype(BF16).astype(F32)

    def queries(q):
        block = xall[q].reshape(half, width + LANES)
        hi = block[:, width : width + 1].astype(F32)
        lo = block[:, width + LANES // 2 : width + LANES // 2 + 1].astype(F32)
        limits = hi * 256.0 + lo
        position = me * keys + lax.broadcasted_iota(jnp.int32, (half, keys), 1)
        mask[q] = jnp.where(position.astype(F32) < limits, 1.0 / (limits + 1.0), 0.0)
        x = block[:, :width]
        for g in range(groups):
            q_all[q, g] = silu(dot(x, w_q[:, g * cols : (g + 1) * cols])).astype(BF16)

    loads[1].wait()
    for d in range(1, chips):
        gathers[d].wait_recv()
        forwards[d].start()
    queries(0)
    for d in range(chips):
        forwards[d].wait_recv()
    queries(1)

    scale = 0.5 * head ** (-0.5)

    def attend(q, g):
        outs = []
        for h in range(heads_in):
            cut = slice(h * head, (h + 1) * head)
            s = lax.dot_general(
                q_all[q, g, :, cut], kv[g, pl.ds(0, keys), cut],
                (((1,), (1,)), ((), ())), preferred_element_type=F32,
            )
            y = s * scale
            weight = ((y * jnp.tanh(y) + y) * mask[q]).astype(BF16)
            outs.append(dot(weight, kv[groups + g, pl.ds(0, keys), cut]))
        return jnp.concatenate(outs, axis=1)

    crosses, directs = [], []
    shifts = {}

    def shifted(q, g, total):
        if g == 0:
            shifts[q] = jnp.mean(total, axis=-1, keepdims=True)
        return total - shifts[q]

    def pass_on(g):
        crosses[g].wait_recv()
        total = shifted(0, g, keep[g] + recv_c[g].astype(F32))
        own[g] = total[:rows]
        send_d[g] = total.reshape(chips, rows, cols).astype(BF16)
        for d in range(1, chips):
            copy = remote(
                send_d.at[g, d], recv_d.at[g, d], rd_s.at[g, d], rd_r.at[g, d], behind(d)
            )
            copy.start()
            directs.append(copy)

    for g in range(groups):
        send_c[g] = shifted(1, g, attend(1, g)).astype(BF16)
        crosses.append(remote(send_c.at[g], recv_c.at[g], rc_s.at[g], rc_r.at[g], sibling))
        crosses[g].start()
        keep[g] = attend(0, g)
        if g > 0:
            pass_on(g - 1)
    pass_on(groups - 1)

    selves = []
    for g in range(groups):
        q_own = q_all[0, g, :rows, :].astype(F32)
        k_own = kv[g, pl.ds(keys, rows), :].astype(F32)
        v_own = kv[groups + g, pl.ds(keys, rows), :].astype(F32)
        product = q_own * k_own
        for h in range(heads_in):
            cut = slice(h * head, (h + 1) * head)
            s = jnp.sum(product[:, cut], axis=-1, keepdims=True) * (head ** (-0.5))
            weight = (silu(s) / count).astype(BF16).astype(F32)
            selves.append(weight * v_own[:, cut])
    self_term = jnp.concatenate(selves, axis=1)
    loads[2].wait()

    k = 0
    sums = []
    for g in range(groups):
        total = own[g]
        for d in range(1, chips):
            directs[k].wait_recv()
            k += 1
            total = total + recv_d[g, d].astype(F32)
        sums.append(total)
    attended = jnp.concatenate(sums, axis=1) + self_term
    mixed = (layer_norm(attended) * gate).astype(BF16)
    out_ref[...] = (cand_ref[...].astype(F32) + dot(mixed, w_out[...])).astype(BF16)

    for d in range(1, chips):
        gathers[d].wait_send()
    for copy in forwards + crosses + directs:
        copy.wait_send()


def solution(mesh):
    n = mesh.shape["hist"]
    chips = n // 2

    def on_device(history, candidates, hist_length, visible, w_proj, w_out):
        keys = history.shape[0]
        rows, width = candidates.shape
        cols = 2 * (width // HEADS)
        groups = width // cols
        half = chips * rows
        dma = pltpu.SemaphoreType.DMA
        return pl.pallas_call(
            functools.partial(kernel, n, cols),
            out_shape=jax.ShapeDtypeStruct((rows, width), BF16),
            in_specs=[
                pl.BlockSpec(memory_space=pl.ANY),
                pl.BlockSpec(memory_space=pltpu.VMEM),
                pl.BlockSpec(memory_space=pltpu.SMEM),
                pl.BlockSpec(memory_space=pltpu.SMEM),
                pl.BlockSpec(memory_space=pl.ANY),
                pl.BlockSpec(memory_space=pl.ANY),
            ],
            out_specs=pl.BlockSpec(memory_space=pltpu.VMEM),
            scratch_shapes=[
                pltpu.VMEM((keys, width), BF16),
                pltpu.VMEM((2 * groups, width, cols), BF16),
                pltpu.VMEM((width, width), BF16),
                pltpu.VMEM((width, width), BF16),
                pltpu.VMEM((width, width), BF16),
                pltpu.VMEM((keys + rows, width), BF16),
                pltpu.VMEM((2 * groups, keys + rows, cols), BF16),
                pltpu.VMEM((2, chips, rows, width + LANES), BF16),
                pltpu.VMEM((2, groups, half, cols), BF16),
                pltpu.VMEM((2, half, keys), F32),
                pltpu.VMEM((groups, half, cols), BF16),
                pltpu.VMEM((groups, half, cols), BF16),
                pltpu.VMEM((groups, half, cols), F32),
                pltpu.VMEM((groups, chips, rows, cols), BF16),
                pltpu.VMEM((groups, chips, rows, cols), BF16),
                pltpu.VMEM((groups, rows, cols), F32),
                dma((4,)),
                dma((2 * groups,)),
                dma((chips,)),
                dma((chips,)),
                dma((chips,)),
                dma((chips,)),
                dma((groups,)),
                dma((groups,)),
                dma((groups, chips)),
                dma((groups, chips)),
            ],
            compiler_params=pltpu.CompilerParams(
                collective_id=0, has_side_effects=True, vmem_limit_bytes=60 * 1024 * 1024
            ),
            name="score",
        )(history, candidates, hist_length, visible, w_proj, w_out)

    return jax.shard_map(
        on_device,
        mesh=mesh,
        in_specs=(
            P(("groups", "hist"), None),
            P(("groups", "hist"), None),
            P("groups"),
            P(("groups", "hist")),
            P(),
            P(),
        ),
        out_specs=P(("groups", "hist"), None),
        check_vma=False,
    )
```

time: 161 us -> 31.1 us (0.19)
  waiting for transfers between devices: 106 us -> 0 us
  matrix products: 38.2 us -> 0 us
  Pallas kernels: 0 us -> 28.8 us
  other arithmetic: 6.28 us -> 0 us
  starting transfers between devices: 5.84 us -> 0 us
    ppermute x48 -> x0, waiting for transfers between devices: 106 us -> none  [shifted(): lax.ppermute(shard, axis, [(i, (i + by) % size) for i in range(size)])]
    dot_general x19 -> x0, matrix products: 38.2 us -> none  [the longest x16 28.7 us: attend(): jnp.einsum('hrk,khd->rhd', weight, v_h, preferred_element_type=jnp.float32)]
    pallas_call x0 -> x1, Pallas kernels: none -> 28.8 us  [on_device(): pl.pallas_call(functools.partial(kernel, n, cols), out_shape=jax.ShapeDty...]
    ppermute x48 -> x0, starting transfers between devices: 5.84 us -> none  [shifted(): lax.ppermute(shard, axis, [(i, (i + by) % size) for i in range(size)])]
    reduce_sum x7 -> x0, other arithmetic: 3.79 us -> none  [the longest x3 2.15 us: layer_norm(): centred = rows - jnp.mean(rows, axis=-1, keepdims=True)]
  transfers between devices with their start and end apart: 48 -> 0, of which waited for: 16 -> 0; matrix products, arithmetic and copies ran while one was open for 0% -> 0% of each run, Pallas kernels for 0% -> 0%
where the time goes in v1:
time: 31.1 us; the launch traced here: 30.8 us
  Pallas kernels  28.8 us (93%)
  local copies, waits for them, and re-layouts  1.38 us (4%)
  between operations  0.66 us (2%)
    pallas_call x1, Pallas kernels, on_device(): pl.pallas_call(functools.partial(kernel, n, cols), out_shape=jax.ShapeDty...  28.8 us
    unnamed x1, local copies, waits for them, and re-layouts  1.38 us

profile of v1, /device:TPU:0, one launch (start us, length us, event | category | flops | bytes accessed | tf_op | source)
XLA Modules:
  0.0 30.8 jit_solution(15272399424162225190)
XLA Ops:
  0.7 28.8 %score.1 = bf16[16,1024]{1,0:T(8,128)(2,1)} custom-call(bf16[512,1024]{1,0:T(8,128)(2,1)} %hist_ref.1, bf16[16,1024]{1,0:T(8,128)(2,1)} %cand_ref.1, s32[1]{0:T(128)S(6)} %copy.8.length_ref, s32[16]{0:T(128)} %visible_ref.1, bf16[1024,4096]{1,0:T(8,128)(2,1)} %w_proj_ref.1, bf16[1024,1024]{1,0:T(8,128)(2,1)} %w_out_ref.1), custom_call_target="tpu_custom_call" | custom-call | tf_op jit(solution)/shard_map/score/pallas_call | solution.py:230
  29.5 1.4 %copy.9 = bf16[16,1024]{1,0:T(8,128)(2,1)} copy(bf16[16,1024]{1,0:T(8,128)(2,1)} %score.1) | data formatting | bytes 65536

commit v2 on v1

--- a/solution.py
+++ b/solution.py
@@ -89,6 +89,10 @@
     xall[0, 0, :, width:] = parts.astype(F32).astype(BF16)
     xs[pl.ds(keys, rows), :] = cand_norm
 
+    load_hist.wait()
+    for r in range(0, keys, LANES):
+        xs[pl.ds(r, LANES), :] = layer_norm(hist[pl.ds(r, LANES), :]).astype(BF16)
+
     pl.semaphore_wait(barrier, chips)
 
     def remote(src, dst, s, r, to):
@@ -109,35 +113,27 @@
         gathers[d].start()
     forwards[0].start()
 
-    load_hist.wait()
-    for r in range(0, keys, LANES):
-        xs[pl.ds(r, LANES), :] = layer_norm(hist[pl.ds(r, LANES), :]).astype(BF16)
     for j in range(2 * groups):
         kv_loads[j].wait()
         kv[j] = silu(dot(xs[...], w_kv[j])).astype(BF16)
 
-    loads[0].wait()
-    gate = silu(dot(xs[pl.ds(keys, rows), :], w_gate[...])).astype(BF16).astype(F32)
-
-    def queries(q):
+    def limits_of(q):
         block = xall[q].reshape(half, width + LANES)
         hi = block[:, width : width + 1].astype(F32)
         lo = block[:, width + LANES // 2 : width + LANES // 2 + 1].astype(F32)
         limits = hi * 256.0 + lo
         position = me * keys + lax.broadcasted_iota(jnp.int32, (half, keys), 1)
         mask[q] = jnp.where(position.astype(F32) < limits, 1.0 / (limits + 1.0), 0.0)
-        x = block[:, :width]
-        for g in range(groups):
-            q_all[q, g] = silu(dot(x, w_q[:, g * cols : (g + 1) * cols])).astype(BF16)
+
+    def query(q, g):
+        x = xall[q, :, :, :width].reshape(half, width)
+        q_all[q, g] = silu(dot(x, w_q[:, g * cols : (g + 1) * cols])).astype(BF16)
 
     loads[1].wait()
     for d in range(1, chips):
         gathers[d].wait_recv()
         forwards[d].start()
-    queries(0)
-    for d in range(chips):
-        forwards[d].wait_recv()
-    queries(1)
+    limits_of(0)
 
     scale = 0.5 * head ** (-0.5)
 
@@ -155,16 +151,14 @@
         return jnp.concatenate(outs, axis=1)
 
     crosses, directs = [], []
-    shifts = {}
-
-    def shifted(q, g, total):
-        if g == 0:
-            shifts[q] = jnp.mean(total, axis=-1, keepdims=True)
-        return total - shifts[q]
+    shifts = []
 
     def pass_on(g):
         crosses[g].wait_recv()
-        total = shifted(0, g, keep[g] + recv_c[g].astype(F32))
+        total = keep[g] + recv_c[g]
+        if g == 0:
+            shifts.append(jnp.mean(total, axis=-1, keepdims=True))
+        total = total - shifts[0]
         own[g] = total[:rows]
         send_d[g] = total.reshape(chips, rows, cols).astype(BF16)
         for d in range(1, chips):
@@ -174,11 +168,21 @@
             copy.start()
             directs.append(copy)
 
+    query(0, 0)
+    keep[0] = attend(0, 0)
+    loads[0].wait()
+    gate = silu(dot(xs[pl.ds(keys, rows), :], w_gate[...])).astype(BF16).astype(F32)
+    for d in range(chips):
+        forwards[d].wait_recv()
+    limits_of(1)
     for g in range(groups):
-        send_c[g] = shifted(1, g, attend(1, g)).astype(BF16)
+        query(1, g)
+        send_c[g] = attend(1, g)
         crosses.append(remote(send_c.at[g], recv_c.at[g], rc_s.at[g], rc_r.at[g], sibling))
         crosses[g].start()
-        keep[g] = attend(0, g)
+        if g + 1 < groups:
+            query(0, g + 1)
+            keep[g + 1] = attend(0, g + 1)
         if g > 0:
             pass_on(g - 1)
     pass_on(groups - 1)
@@ -250,8 +254,8 @@
                 pltpu.VMEM((2, chips, rows, width + LANES), BF16),
                 pltpu.VMEM((2, groups, half, cols), BF16),
                 pltpu.VMEM((2, half, keys), F32),
-                pltpu.VMEM((groups, half, cols), BF16),
-                pltpu.VMEM((groups, half, cols), BF16),
+                pltpu.VMEM((groups, half, cols), F32),
+                pltpu.VMEM((groups, half, cols), F32),
                 pltpu.VMEM((groups, half, cols), F32),
                 pltpu.VMEM((groups, chips, rows, cols), BF16),
                 pltpu.VMEM((groups, chips, rows, cols), BF16),

time: 31.1 us -> 32 us (1.029)
  Pallas kernels: 28.8 us -> 29.7 us
    pallas_call x1, Pallas kernels: 28.8 us -> 29.7 us  [on_device(): pl.pallas_call(functools.partial(kernel, n, cols), out_shape=jax.ShapeDty...]
where the time goes in v2:
time: 32 us; the launch traced here: 31.7 us
  Pallas kernels  29.7 us (93%)
  local copies, waits for them, and re-layouts  1.38 us (4%)
  between operations  0.66 us (2%)
    pallas_call x1, Pallas kernels, on_device(): pl.pallas_call(functools.partial(kernel, n, cols), out_shape=jax.ShapeDty...  29.7 us
    unnamed x1, local copies, waits for them, and re-layouts  1.38 us

profile of v2, /device:TPU:0, one launch (start us, length us, event | category | flops | bytes accessed | tf_op | source)
XLA Modules:
  0.0 31.7 jit_solution(8200281195347380147)
XLA Ops:
  0.7 29.7 %score.1 = bf16[16,1024]{1,0:T(8,128)(2,1)} custom-call(bf16[512,1024]{1,0:T(8,128)(2,1)} %hist_ref.1, bf16[16,1024]{1,0:T(8,128)(2,1)} %cand_ref.1, s32[1]{0:T(128)S(6)} %copy.8.length_ref, s32[16]{0:T(128)} %visible_ref.1, bf16[1024,4096]{1,0:T(8,128)(2,1)} %w_proj_ref.1, bf16[1024,1024]{1,0:T(8,128)(2,1)} %w_out_ref.1), custom_call_target="tpu_custom_call" | custom-call | tf_op jit(solution)/shard_map/score/pallas_call | solution.py:234
  30.4 1.4 %copy.9 = bf16[16,1024]{1,0:T(8,128)(2,1)} copy(bf16[16,1024]{1,0:T(8,128)(2,1)} %score.1) | data formatting | bytes 65536

commit v3 on v1

--- a/solution.py
+++ b/solution.py
@@ -97,6 +97,7 @@
             device_id={"hist": to}, device_id_type=MESH,
         )
 
+    order = sorted(range(1, chips), key=lambda d: abs(d - chips // 2))
     gathers = [None] + [
         remote(xall.at[0, 0], xall.at[0, d], ag_s.at[d], ag_r.at[d], ahead(d))
         for d in range(1, chips)
@@ -105,7 +106,7 @@
         remote(xall.at[0, d], xall.at[1, d], fw_s.at[d], fw_r.at[d], sibling)
         for d in range(chips)
     ]
-    for d in range(1, chips):
+    for d in order:
         gathers[d].start()
     forwards[0].start()
 
@@ -155,19 +156,17 @@
         return jnp.concatenate(outs, axis=1)
 
     crosses, directs = [], []
-    shifts = {}
-
-    def shifted(q, g, total):
-        if g == 0:
-            shifts[q] = jnp.mean(total, axis=-1, keepdims=True)
-        return total - shifts[q]
+    shifts = []
 
     def pass_on(g):
         crosses[g].wait_recv()
-        total = shifted(0, g, keep[g] + recv_c[g].astype(F32))
+        total = keep[g] + recv_c[g]
+        if g == 0:
+            shifts.append(jnp.mean(total, axis=-1, keepdims=True))
+        total = total - shifts[0]
         own[g] = total[:rows]
         send_d[g] = total.reshape(chips, rows, cols).astype(BF16)
-        for d in range(1, chips):
+        for d in order:
             copy = remote(
                 send_d.at[g, d], recv_d.at[g, d], rd_s.at[g, d], rd_r.at[g, d], behind(d)
             )
@@ -175,7 +174,7 @@
             directs.append(copy)
 
     for g in range(groups):
-        send_c[g] = shifted(1, g, attend(1, g)).astype(BF16)
+        send_c[g] = attend(1, g)
         crosses.append(remote(send_c.at[g], recv_c.at[g], rc_s.at[g], rc_r.at[g], sibling))
         crosses[g].start()
         keep[g] = attend(0, g)
@@ -201,7 +200,7 @@
     sums = []
     for g in range(groups):
         total = own[g]
-        for d in range(1, chips):
+        for d in order:
             directs[k].wait_recv()
             k += 1
             total = total + recv_d[g, d].astype(F32)
@@ -250,8 +249,8 @@
                 pltpu.VMEM((2, chips, rows, width + LANES), BF16),
                 pltpu.VMEM((2, groups, half, cols), BF16),
                 pltpu.VMEM((2, half, keys), F32),
-                pltpu.VMEM((groups, half, cols), BF16),
-                pltpu.VMEM((groups, half, cols), BF16),
+                pltpu.VMEM((groups, half, cols), F32),
+                pltpu.VMEM((groups, half, cols), F32),
                 pltpu.VMEM((groups, half, cols), F32),
                 pltpu.VMEM((groups, chips, rows, cols), BF16),
                 pltpu.VMEM((groups, chips, rows, cols), BF16),

time: 31.1 us -> 30.8 us (level)
  no operation moved by 1% of the time
where the time goes in v3:
time: 30.8 us; the launch traced here: 30.5 us
  Pallas kernels  28.5 us (93%)
  local copies, waits for them, and re-layouts  1.38 us (4%)
  between operations  0.66 us (2%)
    pallas_call x1, Pallas kernels, on_device(): pl.pallas_call(functools.partial(kernel, n, cols), out_shape=jax.ShapeDty...  28.5 us
    unnamed x1, local copies, waits for them, and re-layouts  1.38 us

profile of v3, /device:TPU:0, one launch (start us, length us, event | category | flops | bytes accessed | tf_op | source)
XLA Modules:
  0.0 30.5 jit_solution(6882926381119707882)
XLA Ops:
  0.7 28.5 %score.1 = bf16[16,1024]{1,0:T(8,128)(2,1)} custom-call(bf16[512,1024]{1,0:T(8,128)(2,1)} %hist_ref.1, bf16[16,1024]{1,0:T(8,128)(2,1)} %cand_ref.1, s32[1]{0:T(128)S(6)} %copy.8.length_ref, s32[16]{0:T(128)} %visible_ref.1, bf16[1024,4096]{1,0:T(8,128)(2,1)} %w_proj_ref.1, bf16[1024,1024]{1,0:T(8,128)(2,1)} %w_out_ref.1), custom_call_target="tpu_custom_call" | custom-call | tf_op jit(solution)/shard_map/score/pallas_call | solution.py:229
  29.2 1.4 %copy.9 = bf16[16,1024]{1,0:T(8,128)(2,1)} copy(bf16[16,1024]{1,0:T(8,128)(2,1)} %score.1) | data formatting | bytes 65536

commit v4 on v3

--- a/solution.py
+++ b/solution.py
@@ -156,16 +156,12 @@
         return jnp.concatenate(outs, axis=1)
 
     crosses, directs = [], []
-    shifts = []
 
     def pass_on(g):
         crosses[g].wait_recv()
         total = keep[g] + recv_c[g]
-        if g == 0:
-            shifts.append(jnp.mean(total, axis=-1, keepdims=True))
-        total = total - shifts[0]
         own[g] = total[:rows]
-        send_d[g] = total.reshape(chips, rows, cols).astype(BF16)
+        send_d[g] = total.reshape(chips, rows, cols)
         for d in order:
             copy = remote(
                 send_d.at[g, d], recv_d.at[g, d], rd_s.at[g, d], rd_r.at[g, d], behind(d)
@@ -203,7 +199,7 @@
         for d in order:
             directs[k].wait_recv()
             k += 1
-            total = total + recv_d[g, d].astype(F32)
+            total = total + recv_d[g, d]
         sums.append(total)
     attended = jnp.concatenate(sums, axis=1) + self_term
     mixed = (layer_norm(attended) * gate).astype(BF16)
@@ -252,8 +248,8 @@
                 pltpu.VMEM((groups, half, cols), F32),
                 pltpu.VMEM((groups, half, cols), F32),
                 pltpu.VMEM((groups, half, cols), F32),
-                pltpu.VMEM((groups, chips, rows, cols), BF16),
-                pltpu.VMEM((groups, chips, rows, cols), BF16),
+                pltpu.VMEM((groups, chips, rows, cols), F32),
+                pltpu.VMEM((groups, chips, rows, cols), F32),
                 pltpu.VMEM((groups, rows, cols), F32),
                 dma((4,)),
                 dma((2 * groups,)),

time: 30.8 us -> 35.4 us (1.15)
  Pallas kernels: 28.5 us -> 33.2 us
    pallas_call x1, Pallas kernels: 28.5 us -> 33.2 us  [on_device(): pl.pallas_call(functools.partial(kernel, n, cols), out_shape=jax.ShapeDty...]
where the time goes in v4:
time: 35.4 us; the launch traced here: 35.2 us
  Pallas kernels  33.2 us (94%)
  local copies, waits for them, and re-layouts  1.38 us (4%)
  between operations  0.66 us (2%)
    pallas_call x1, Pallas kernels, on_device(): pl.pallas_call(functools.partial(kernel, n, cols), out_shape=jax.ShapeDty...  33.2 us
    unnamed x1, local copies, waits for them, and re-layouts  1.38 us

profile of v4, /device:TPU:0, one launch (start us, length us, event | category | flops | bytes accessed | tf_op | source)
XLA Modules:
  0.0 35.2 jit_solution(13732238029564568191)
XLA Ops:
  0.7 33.2 %score.1 = bf16[16,1024]{1,0:T(8,128)(2,1)} custom-call(bf16[512,1024]{1,0:T(8,128)(2,1)} %hist_ref.1, bf16[16,1024]{1,0:T(8,128)(2,1)} %cand_ref.1, s32[1]{0:T(128)S(6)} %copy.8.length_ref, s32[16]{0:T(128)} %visible_ref.1, bf16[1024,4096]{1,0:T(8,128)(2,1)} %w_proj_ref.1, bf16[1024,1024]{1,0:T(8,128)(2,1)} %w_out_ref.1), custom_call_target="tpu_custom_call" | custom-call | tf_op jit(solution)/shard_map/score/pallas_call | solution.py:225
  33.8 1.4 %copy.9 = bf16[16,1024]{1,0:T(8,128)(2,1)} copy(bf16[16,1024]{1,0:T(8,128)(2,1)} %score.1) | data formatting | bytes 65536
